TPU v7x, 128 devices: a whole 4x4x4 slice. The times are simulated.
128 devices in a mesh: blk: 32 (over x, z, y_hi), quarter: 4 (over y_lo, core).
Axes of the slice: x: 4, y: 4 (y_hi: 2, y_lo: 2; y = y_hi * 2 + y_lo), z: 4, core: 2. Of those that a mesh axis runs over, the one named last changes fastest.
Arguments:
- bints: bfloat16 [256, 512, 1280], P('blk', None, 'quarter'), may hold values from -2.5 to 2.5
- occ_energy: float32 [256], replicated, may hold values from -2 to -0.5
- vir_energy: float32 [512], replicated, may hold values from 0.2 to 3
Outputs:
- gamma: float32 [256, 512, 1280], P(('blk', 'quarter'))
- vvdens: float32 [512, 512], P(('blk', 'quarter'))
All inputs are finite; a program needn't handle non-finite values.
Results may differ from a plain program's by a relative error of at most 0.0016.
Values may be sent and summed in bfloat16 or wider, within the bound.
A program may use at most 128 MiB of HBM per device.

v0:
```python
import jax
import jax.numpy as jnp
from jax import lax
from jax.sharding import PartitionSpec as P

V = 512
CYCLE = 3


def shifted(shard, axis, by):
    devices = lax.axis_size(axis)
    return lax.ppermute(shard, axis, [(i, (i + by) % devices) for i in range(devices)])


def per_device(bints, occ_energy, vir_energy):
    local = lax.all_to_all(bints, "quarter", split_axis=0, concat_axis=2, tiled=True)
    quarters = lax.axis_size("quarter")
    block_count = lax.axis_size("blk")
    block_id = lax.axis_index("blk")
    quarter_id = lax.axis_index("quarter")
    occ_rows = local.shape[0]
    own_group = block_id * quarters + quarter_id
    own_energy = lax.dynamic_slice_in_dim(occ_energy, own_group * occ_rows, occ_rows)
    density = jnp.zeros(local.shape, jnp.float32)
    vv_part = jnp.zeros((V, V), jnp.float32)
    partner_block = local
    for step in range(CYCLE):
        if step > 0:
            partner_block = shifted(partner_block, "blk", 1)
        partner = (block_id - step) % block_count * quarters + quarter_id
        other_energy = lax.dynamic_slice_in_dim(occ_energy, partner * occ_rows, occ_rows)
        pairint = jnp.einsum(
            "iap,jbp->ijab", local, partner_block, preferred_element_type=jnp.float32
        )
        denom = (
            vir_energy[None, None, :, None]
            + vir_energy[None, None, None, :]
            - own_energy[:, None, None, None]
            - other_energy[None, :, None, None]
        )
        amp = pairint / denom
        amp_b = amp.astype(jnp.bfloat16)
        tilde = (2.0 * amp - jnp.swapaxes(amp, 2, 3)).astype(jnp.bfloat16)
        density = density + jnp.einsum(
            "ijab,jbp->iap", tilde, partner_block, preferred_element_type=jnp.float32
        )
        vv_part = vv_part + jnp.einsum(
            "ijac,ijbc->ab", amp_b, tilde, preferred_element_type=jnp.float32
        )
    row_count = V // (block_count * quarters)
    summed = lax.psum(vv_part, ("blk", "quarter"))
    rows_out = lax.dynamic_slice_in_dim(summed, own_group * row_count, row_count, 0)
    return (density, rows_out / PAIRS_SCALE(occ_rows, block_count, quarters))


def PAIRS_SCALE(occ_rows, block_count, quarters):
    return float(occ_rows * block_count * quarters * CYCLE * occ_rows)


def solution(mesh):
    return jax.shard_map(
        per_device,
        mesh=mesh,
        in_specs=(P("blk", None, "quarter"), P(), P()),
        out_specs=(P(("blk", "quarter"), None, None), P(("blk", "quarter"), None)),
        check_vma=False,
    )
```

profile of v0, /device:TPU:1, one launch (start us, length us, event | category | flops | bytes accessed | tf_op | source)
XLA Modules:
  0.0 359.4 jit_solution(8892862195207607736)
XLA Ops:
  7.2 0.0 all-reduce.2.cloned.1.call-start
  7.2 35.3 %all_to_all.18 = bf16[8,512,320]{1,2,0:T(8,128)(2,1)S(1)} all-to-all(bf16[8,512,320]{1,2,0:T(8,128)(2,1)} %param.3), channel_id=1, replica_groups=mesh['blk'=32,'quarter'=4] {'quarter'}, dimensions={0} | all-to-all | bytes 5242880 | tf_op jit(solution)/shard_map/all_to_all | solution.py:16
  42.5 0.0 copy-start
  42.5 0.2 copy.21
  42.6 1.3 copy-done
  44.0 0.0 copy-start.9
  44.0 0.0 copy-start.8
  44.0 2.6 copy.25
  46.5 3.0 collective-permute-start
  49.6 62.2 %collective-permute-done = bf16[2,512,1280]{2,1,0:T(8,128)(2,1)} collective-permute-done((bf16[2,512,1280]{2,1,0:T(8,128)(2,1)}, bf16[2,512,1280]{2,1,0:T(8,128)(2,1)}, u32[]{:S(2)}, u32[]{:S(2)}) %collective-permute-start) | collective-permute-done | bytes 2621472 | tf_op jit(solution)/shard_map/ppermute | solution.py:12
  111.7 0.0 collective-permute-start.1
  111.7 0.0 copy-done.9
  111.8 0.0 copy-start.1
  111.8 0.1 fusion.54
  111.8 0.0 copy-done.8
  111.8 0.1 broadcast_add_fusion
  112.0 1.7 broadcast_subtract_fusion
  113.6 0.3 copy-done.1
  113.9 4.5 %fusion.13 = f32[2,512,2,512,1]{3,1,4,2,0:T(8,128)} fusion(bf16[4,2,512,320]{2,3,1,0:T(8,128)(2,1)S(1)} %bitcast.95), kind=kOutput, calls=%fused_computation.21 | convolution fusion | flops 2684354560 | bytes 6815744 | tf_op jit(solution)/shard_map/iap,jbp->ijab/dot_general | solution.py:32
  118.4 5.2 %copy.22 = f32[2,512,2,512]{1,3,2,0:T(8,128)} copy(f32[2,512,2,512]{3,1,2,0:T(8,128)} %bitcast.89) | data formatting | bytes 8388608 | tf_op jit(solution)/shard_map/iap,jbp->ijab/dot_general | solution.py:32
  123.6 6.2 %fusion.11 = f32[2,512,2,512]{3,1,2,0:T(8,128)} fusion(bf16[2,512,1280,1]{1,2,0,3:T(8,128)(2,1)S(1)} %bitcast.91, bf16[2,512,1280]{2,1,0:T(8,128)(2,1)} %collective-permute-done), kind=kOutput, calls=%fused_computation.19 | convolution fusion | flops 2684354560 | bytes 9437184 | tf_op jit(solution)/shard_map/iap,jbp->ijab/dot_general | solution.py:32
  129.8 5.3 %copy.27 = f32[2,512,2,512]{1,3,2,0:T(8,128)} copy(f32[2,512,2,512]{3,1,2,0:T(8,128)} %fusion.11) | data formatting | bytes 8388608 | tf_op jit(solution)/shard_map/iap,jbp->ijab/dot_general | solution.py:32
  135.1 39.5 %collective-permute-done.1 = bf16[2,512,1280]{2,1,0:T(8,128)(2,1)} collective-permute-done((bf16[2,512,1280]{2,1,0:T(8,128)(2,1)}, bf16[2,512,1280]{2,1,0:T(8,128)(2,1)}, u32[]{:S(2)}, u32[]{:S(2)}) %collective-permute-start.1) | collective-permute-done | bytes 2621472 | tf_op jit(solution)/shard_map/ppermute | solution.py:12
  174.6 6.1 %fusion.7 = f32[2,512,2,512]{3,1,2,0:T(8,128)} fusion(bf16[2,512,1280,1]{1,2,0,3:T(8,128)(2,1)S(1)} %bitcast.92, bf16[2,512,1280]{2,1,0:T(8,128)(2,1)} %collective-permute-done.1), kind=kOutput, calls=%fused_computation.15 | convolution fusion | flops 2684354560 | bytes 9437184 | tf_op jit(solution)/shard_map/iap,jbp->ijab/dot_general | solution.py:32
  180.7 5.2 %copy.30 = f32[2,512,2,512]{1,3,2,0:T(8,128)} copy(f32[2,512,2,512]{3,1,2,0:T(8,128)} %fusion.7) | data formatting | bytes 8388608 | tf_op jit(solution)/shard_map/iap,jbp->ijab/dot_general | solution.py:32
  185.9 12.9 %fusion.52 = (bf16[2,2,512,512]{3,2,0,1:T(8,128)(2,1)S(1)}, bf16[2,2,512,512]{3,2,0,1:T(8,128)(2,1)S(1)}, bf16[2,2,512,512]{3,2,0,1:T(8,128)(2,1)S(1)}, bf16[2,2...) fusion(f32[2]{0:T(128)S(1)} %get-tuple-element.12, ...), kind=kLoop, calls=%fused_computation.42 | loop fusion | flops 22020096 | bytes 39845912 | tf_op jit(solution)/shard_map/convert_element_type | solution.py:42
  198.8 0.0 copy-start.6
  198.8 0.0 copy-start.4
  198.8 0.0 copy-start.2
  198.9 0.0 copy-start.7
  198.9 4.6 %fusion.25 = f32[512,512]{1,0:T(8,128)S(1)} fusion(bf16[2,2,512,512]{3,2,0,1:T(8,128)(2,1)S(1)} %get-tuple-element.10, bf16[2,2,512,512]{3,2,0,1:T(8,128)(2,1)} %get-tuple-element.11), kind=kOutput, calls=%fused_computation.33 | convolution fusion | flops 1073741824 | bytes 5242880 | tf_op jit(solution)/shard_map/ijac,ijbc->ab/dot_general | solution.py:47
  203.4 0.0 copy-done.6
  203.5 0.0 copy-done.4
  203.5 0.0 copy-done.7
  203.5 1.3 fusion.45
  204.8 0.0 copy-done.2
  204.8 2.3 fusion.40
  207.1 0.0 all-reduce.2.cloned.1.call-update
  207.1 0.0 copy-start.5
  207.1 4.6 %fusion.55 = f32[2,512,1280,1]{2,1,0,3:T(8,128)S(1)} fusion(bf16[2,2,512,512]{3,2,0,1:T(8,128)(2,1)} %copy-done.6, bf16[2,512,1280,1]{1,2,3,0:T(8,128)(2,1)S(1)} %bitcast.93), kind=kOutput, calls=%fused_computation.46 | convolution fusion | flops 2684354560 | bytes 9961472 | tf_op jit(solution)/shard_map/ijab,jbp->iap/dot_general | solution.py:44
  211.7 0.0 copy-done.5
  211.7 0.0 copy-start.3
  211.8 4.8 %fusion.9 = f32[2,512,1280,1]{2,1,0,3:T(8,128)S(1)} fusion(bf16[2,2,512,512]{3,2,0,1:T(8,128)(2,1)S(1)} %copy-done.5, bf16[2,512,1280]{2,1,0:T(8,128)(2,1)} %collective-permute-done), kind=kOutput, calls=%fused_computation.17 | convolution fusion | flops 2684354560 | bytes 9961472 | tf_op jit(solution)/shard_map/ijab,jbp->iap/dot_general | solution.py:44
  216.5 0.0 copy-done.3
  216.5 6.3 %bitcast_add_fusion = f32[2,512,1280]{2,1,0:T(8,128)} fusion(f32[2,512,1280,1]{2,1,0,3:T(8,128)S(1)} %fusion.9, f32[2,512,1280,1]{2,1,0,3:T(8,128)S(1)} %fusion.55, bf16[2,2,512,512]{3,2,0,1:T(8,128)(2,1)S(1)} %copy-done.3, bf16[2,512,1280]{2,1,0:T(8,128)(2,1)} %collective-permute-done.1), kind=kOutput, calls=%fused_computation.6 | convolution fusion | flops 2686976000 | bytes 20447232 | tf_op jit(solution)/shard_map/ijab,jbp->iap/dot_general | solution.py:44
  222.9 128.3 %all-reduce.2.cloned.1.call-done = f32[512,512]{1,0:T(8,128)} async-done(((f32[512,512]{1,0:T(8,128)}), f32[512,512]{1,0:T(8,128)}) %all-reduce.2.cloned.1.call-update) | async-done | bytes 1048592 | tf_op jit(solution)/shard_map/psum | solution.py:51
  351.2 1.3 dynamic-slice_multiply_fusion
Async XLA Ops:
  7.2 344.1 %all-reduce.2.cloned.1.call-start = ((), (), s32[]{:S(2)}) async-start(), calls=%async_computation.1 | async-start | bytes 2097152 | tf_op jit(solution)/shard_map/psum | solution.py:51
  42.5 1.5 copy-start
  44.0 67.8 %copy-start.9 = (f32[256]{0:T(256)S(1)}, f32[256]{0:T(256)}, u32[]{:S(2)}) copy-start(f32[256]{0:T(256)} %param.4) | copy-start | bytes 3076
  44.0 67.9 %copy-start.8 = (f32[512]{0:T(512)S(1)}, f32[512]{0:T(512)}, u32[]{:S(2)}) copy-start(f32[512]{0:T(512)} %param.5) | copy-start | bytes 6148
  46.5 65.2 %collective-permute-start = (bf16[2,512,1280]{2,1,0:T(8,128)(2,1)}, bf16[2,512,1280]{2,1,0:T(8,128)(2,1)}, u32[]{:S(2)}, u32[]{:S(2)}) collective-permute-start(bf16[2,512,1280]{2,1,0:T(8,128)(2,1)} %copy.25), channel_id=1, source_target_pairs={{0,4},{4,8},{8,12},{12,16},{16,20},{20,24},{24,28},{28,32},{32,36}... | collective-permute-start | bytes 7864328 | tf_op jit(solution)/shard_map/ppermute | solution.py:12
  111.7 62.8 %collective-permute-start.1 = (bf16[2,512,1280]{2,1,0:T(8,128)(2,1)}, bf16[2,512,1280]{2,1,0:T(8,128)(2,1)}, u32[]{:S(2)}, u32[]{:S(2)}) collective-permute-start(bf16[2,512,1280]{2,1,0:T(8,128)(2,1)} %collective-permute-done), channel_id=1, source_target_pairs={{0,4},{4,8},{8,12},{12,16},{16,20},{20,24},{24,28},{28,32},{32,36}... | collective-permute-start | bytes 7864328 | tf_op jit(solution)/shard_map/ppermute | solution.py:12
  111.8 2.2 copy-start.1
  198.8 4.6 %copy-start.6 = (bf16[2,2,512,512]{3,2,0,1:T(8,128)(2,1)}, bf16[2,2,512,512]{3,2,0,1:T(8,128)(2,1)S(1)}, u32[]{:S(2)}) copy-start(bf16[2,2,512,512]{3,2,0,1:T(8,128)(2,1)S(1)} %get-tuple-element.10) | copy-start | bytes 6291460
  198.8 4.6 %copy-start.4 = (bf16[2,2,512,512]{3,2,0,1:T(8,128)(2,1)}, bf16[2,2,512,512]{3,2,0,1:T(8,128)(2,1)S(1)}, u32[]{:S(2)}) copy-start(bf16[2,2,512,512]{3,2,0,1:T(8,128)(2,1)S(1)} %get-tuple-element.8) | copy-start | bytes 6291460
  198.8 5.9 %copy-start.2 = (bf16[2,2,512,512]{3,2,0,1:T(8,128)(2,1)}, bf16[2,2,512,512]{3,2,0,1:T(8,128)(2,1)S(1)}, u32[]{:S(2)}) copy-start(bf16[2,2,512,512]{3,2,0,1:T(8,128)(2,1)S(1)} %get-tuple-element.3) | copy-start | bytes 6291460
  198.9 4.6 %copy-start.7 = (bf16[2,2,512,512]{3,2,0,1:T(8,128)(2,1)S(1)}, bf16[2,2,512,512]{3,2,0,1:T(8,128)(2,1)}, u32[]{:S(2)}) copy-start(bf16[2,2,512,512]{3,2,0,1:T(8,128)(2,1)} %get-tuple-element.9) | copy-start | bytes 6291460
  207.1 4.7 %copy-start.5 = (bf16[2,2,512,512]{3,2,0,1:T(8,128)(2,1)S(1)}, bf16[2,2,512,512]{3,2,0,1:T(8,128)(2,1)}, u32[]{:S(2)}) copy-start(bf16[2,2,512,512]{3,2,0,1:T(8,128)(2,1)} %copy-done.4) | copy-start | bytes 6291460
  211.7 4.8 %copy-start.3 = (bf16[2,2,512,512]{3,2,0,1:T(8,128)(2,1)S(1)}, bf16[2,2,512,512]{3,2,0,1:T(8,128)(2,1)}, u32[]{:S(2)}) copy-start(bf16[2,2,512,512]{3,2,0,1:T(8,128)(2,1)} %copy-done.2) | copy-start | bytes 6291460
Sparse Core Ops, SparseCore 0:
  207.2 143.9 all-reduce.1
where the time goes:
time: 360 us; the launch traced here: 359 us
  waiting for transfers between devices  230 us (64%)
  matrix products  40.6 us (11%)
  blocking collectives  35.3 us (10%)
  local copies, waits for them, and re-layouts  20.2 us (6%)
  other arithmetic  16 us (4%)
  between operations  14.2 us (4%)
    psum x1, waiting for transfers between devices, per_device(): summed = lax.psum(vv_part, ('blk', 'quarter'))  128 us
    ppermute x2, waiting for transfers between devices, shifted(): lax.ppermute(shard, axis, [(i, (i + by) % devices) for i in range(devices)])  102 us
    all_to_all x1, blocking collectives, per_device(): lax.all_to_all(bints, 'quarter', split_axis=0, concat_axis=2, tiled=True)  35.3 us
    dot_general x3, matrix products, per_device(): jnp.einsum('iap,jbp->ijab', local, partner_block, preferred_element_type=...  16.8 us
    dot_general x3, local copies, waits for them, and re-layouts, per_device(): jnp.einsum('iap,jbp->ijab', local, partner_block, preferred_element_type=...  15.8 us
    dot_general x3, matrix products, per_device(): jnp.einsum('ijab,jbp->iap', tilde, partner_block, preferred_element_type=...  15.7 us
    convert_element_type x1, other arithmetic, per_device(): amp_b = amp.astype(jnp.bfloat16)  12.9 us
    dot_general x3, matrix products, per_device(): jnp.einsum('ijac,ijbc->ab', amp_b, tilde, preferred_element_type=jnp.floa...  8.13 us
  transfers between devices with their start and end apart: 3, of which 3 were waited for; matrix products, arithmetic and copies ran while one was open for 11% of the time, Pallas kernels for 0%

commit v1 on v0

--- a/solution.py
+++ b/solution.py
@@ -2,6 +2,7 @@
 import jax.numpy as jnp
 from jax import lax
 from jax.sharding import PartitionSpec as P
+from jax.lax import psum
 
 V = 512
 CYCLE = 3
@@ -48,7 +49,7 @@
             "ijac,ijbc->ab", amp_b, tilde, preferred_element_type=jnp.float32
         )
     row_count = V // (block_count * quarters)
-    summed = lax.psum(vv_part, ("blk", "quarter"))
+    summed = psum(psum(vv_part, axis_name="quarter"), axis_name="blk")
     rows_out = lax.dynamic_slice_in_dim(summed, own_group * row_count, row_count, 0)
     return (density, rows_out / PAIRS_SCALE(occ_rows, block_count, quarters))
 

time: 360 us -> 610 us (1.69)
  the two profiles are of different devices: /device:TPU:1 before, /device:TPU:0 now
where the time goes in v1:
time: 610 us; the launch traced here: 609 us
  waiting for transfers between devices  474 us (78%)
  matrix products  46.2 us (8%)
  blocking collectives  34.9 us (6%)
  local copies, waits for them, and re-layouts  20.2 us (3%)
  other arithmetic  16 us (3%)
  between operations  14.1 us (2%)
    psum x2, waiting for transfers between devices, per_device(): summed = psum(psum(vv_part, axis_name='quarter'), axis_name='blk')  371 us
    ppermute x2, waiting for transfers between devices, shifted(): lax.ppermute(shard, axis, [(i, (i + by) % devices) for i in range(devices)])  103 us
    all_to_all x1, blocking collectives, per_device(): lax.all_to_all(bints, 'quarter', split_axis=0, concat_axis=2, tiled=True)  34.9 us
    dot_general x3, matrix products, per_device(): jnp.einsum('ijab,jbp->iap', tilde, partner_block, preferred_element_type=...  21.3 us
    dot_general x3, matrix products, per_device(): jnp.einsum('iap,jbp->ijab', local, partner_block, preferred_element_type=...  16.8 us
    dot_general x3, local copies, waits for them, and re-layouts, per_device(): jnp.einsum('iap,jbp->ijab', local, partner_block, preferred_element_type=...  15.8 us
    convert_element_type x1, other arithmetic, per_device(): amp_b = amp.astype(jnp.bfloat16)  12.9 us
  transfers between devices with their start and end apart: 4, of which 4 were waited for; matrix products, arithmetic and copies ran while one was open for 7% of the time, Pallas kernels for 0%

profile of v1, /device:TPU:0, one launch (start us, length us, event | category | flops | bytes accessed | tf_op | source)
XLA Modules:
  0.0 609.4 jit_solution(6891630874351233915)
XLA Ops:
  7.2 0.0 all-reduce.3.cloned.1.call-start
  7.2 34.9 %all_to_all.18 = bf16[8,512,320]{1,2,0:T(8,128)(2,1)S(1)} all-to-all(bf16[8,512,320]{1,2,0:T(8,128)(2,1)} %param.3), channel_id=1, replica_groups=mesh['blk'=32,'quarter'=4] {'quarter'}, dimensions={0} | all-to-all | bytes 5242880 | tf_op jit(solution)/shard_map/all_to_all | solution.py:17
  42.1 0.0 copy-start
  42.1 0.2 copy.21
  42.3 1.3 copy-done
  43.6 0.0 copy-start.9
  43.6 0.0 copy-start.8
  43.6 2.6 copy.25
  46.2 3.3 collective-permute-start
  49.5 62.5 %collective-permute-done = bf16[2,512,1280]{2,1,0:T(8,128)(2,1)} collective-permute-done((bf16[2,512,1280]{2,1,0:T(8,128)(2,1)}, bf16[2,512,1280]{2,1,0:T(8,128)(2,1)}, u32[]{:S(2)}, u32[]{:S(2)}) %collective-permute-start) | collective-permute-done | bytes 2621472 | tf_op jit(solution)/shard_map/ppermute | solution.py:13
  112.0 0.0 collective-permute-start.1
  112.0 0.0 copy-done.9
  112.0 0.0 copy-start.1
  112.0 0.1 fusion.54
  112.1 0.0 copy-done.8
  112.1 0.1 broadcast_add_fusion
  112.2 1.7 broadcast_subtract_fusion
  113.9 0.3 copy-done.1
  114.2 4.5 fusion.13
  118.6 5.2 copy.22
  123.9 6.2 %fusion.11 = f32[2,512,2,512]{3,1,2,0:T(8,128)} fusion(bf16[2,512,1280,1]{1,2,0,3:T(8,128)(2,1)S(1)} %bitcast.91, bf16[2,512,1280]{2,1,0:T(8,128)(2,1)} %collective-permute-done), kind=kOutput, calls=%fused_computation.19 | convolution fusion | flops 2684354560 | bytes 9437184 | tf_op jit(solution)/shard_map/iap,jbp->ijab/dot_general | solution.py:33
  130.1 5.3 copy.27
  135.3 40.3 %collective-permute-done.1 = bf16[2,512,1280]{2,1,0:T(8,128)(2,1)} collective-permute-done((bf16[2,512,1280]{2,1,0:T(8,128)(2,1)}, bf16[2,512,1280]{2,1,0:T(8,128)(2,1)}, u32[]{:S(2)}, u32[]{:S(2)}) %collective-permute-start.1) | collective-permute-done | bytes 2621472 | tf_op jit(solution)/shard_map/ppermute | solution.py:13
  175.7 6.1 %fusion.7 = f32[2,512,2,512]{3,1,2,0:T(8,128)} fusion(bf16[2,512,1280,1]{1,2,0,3:T(8,128)(2,1)S(1)} %bitcast.92, bf16[2,512,1280]{2,1,0:T(8,128)(2,1)} %collective-permute-done.1), kind=kOutput, calls=%fused_computation.15 | convolution fusion | flops 2684354560 | bytes 9437184 | tf_op jit(solution)/shard_map/iap,jbp->ijab/dot_general | solution.py:33
  181.8 5.2 copy.30
  187.0 12.9 %fusion.52 = (bf16[2,2,512,512]{3,2,0,1:T(8,128)(2,1)S(1)}, bf16[2,2,512,512]{3,2,0,1:T(8,128)(2,1)S(1)}, bf16[2,2,512,512]{3,2,0,1:T(8,128)(2,1)S(1)}, bf16[2,2...) fusion(f32[2]{0:T(128)S(1)} %get-tuple-element.12, ...), kind=kLoop, calls=%fused_computation.42 | loop fusion | flops 22020096 | bytes 39845912 | tf_op jit(solution)/shard_map/convert_element_type | solution.py:43
  199.9 0.0 copy-start.6
  199.9 0.0 copy-start.4
  199.9 0.0 copy-start.2
  200.0 0.0 copy-start.7
  200.0 4.6 fusion.25
  204.5 0.0 copy-done.6
  204.5 0.0 copy-done.4
  204.6 0.0 copy-done.7
  204.6 1.3 fusion.45
  205.8 0.0 copy-done.2
  205.9 2.3 fusion.40
  208.1 0.0 all-reduce.3.cloned.1.call-update
  208.1 0.2 all-reduce.5.cloned.1.call-start
  208.4 0.0 copy-start.5
  208.4 7.0 %fusion.55 = f32[2,512,1280,1]{2,1,0,3:T(8,128)} fusion(bf16[2,2,512,512]{3,2,0,1:T(8,128)(2,1)} %copy-done.6, bf16[2,512,1280,1]{1,2,3,0:T(8,128)(2,1)S(1)} %bitcast.93), kind=kOutput, calls=%fused_computation.46 | convolution fusion | flops 2684354560 | bytes 9961472 | tf_op jit(solution)/shard_map/ijab,jbp->iap/dot_general | solution.py:45
  215.3 0.0 copy-done.5
  215.3 0.0 copy-start.3
  215.4 6.5 %fusion.9 = f32[2,512,1280,1]{2,1,0,3:T(8,128)} fusion(bf16[2,2,512,512]{3,2,0,1:T(8,128)(2,1)S(1)} %copy-done.5, bf16[2,512,1280]{2,1,0:T(8,128)(2,1)} %collective-permute-done), kind=kOutput, calls=%fused_computation.17 | convolution fusion | flops 2684354560 | bytes 9961472 | tf_op jit(solution)/shard_map/ijab,jbp->iap/dot_general | solution.py:45
  221.8 21.5 %all-reduce.3.cloned.1.call-done = f32[512,512]{1,0:T(8,128)} async-done(((f32[512,512]{1,0:T(8,128)}), f32[512,512]{1,0:T(8,128)}) %all-reduce.3.cloned.1.call-update) | async-done | bytes 1048592 | tf_op jit(solution)/shard_map/psum | solution.py:52
  243.4 0.0 all-reduce.5.cloned.1.call-update
  243.4 0.0 copy-done.3
  243.4 7.9 %bitcast_add_fusion = f32[2,512,1280]{2,1,0:T(8,128)} fusion(f32[2,512,1280,1]{2,1,0,3:T(8,128)} %fusion.9, f32[2,512,1280,1]{2,1,0,3:T(8,128)} %fusion.55, bf16[2,2,512,512]{3,2,0,1:T(8,128)(2,1)S(1)} %copy-done.3, bf16[2,512,1280]{2,1,0:T(8,128)(2,1)} %collective-permute-done.1), kind=kOutput, calls=%fused_computation.6 | convolution fusion | flops 2686976000 | bytes 20447232 | tf_op jit(solution)/shard_map/ijab,jbp->iap/dot_general | solution.py:45
  251.3 349.9 %all-reduce.5.cloned.1.call-done = f32[512,512]{1,0:T(8,128)} async-done(((f32[512,512]{1,0:T(8,128)}), f32[512,512]{1,0:T(8,128)}) %all-reduce.5.cloned.1.call-update) | async-done | bytes 1048592 | tf_op jit(solution)/shard_map/psum | solution.py:52
  601.2 1.3 dynamic-slice_multiply_fusion
Async XLA Ops:
  7.2 236.2 %all-reduce.3.cloned.1.call-start = ((), (), s32[]{:S(2)}) async-start(), calls=%async_computation.1 | async-start | bytes 2097152 | tf_op jit(solution)/shard_map/psum | solution.py:52
  42.1 1.5 copy-start
  43.6 68.4 %copy-start.9 = (f32[256]{0:T(256)S(1)}, f32[256]{0:T(256)}, u32[]{:S(2)}) copy-start(f32[256]{0:T(256)} %param.4) | copy-start | bytes 3076
  43.6 68.4 %copy-start.8 = (f32[512]{0:T(512)S(1)}, f32[512]{0:T(512)}, u32[]{:S(2)}) copy-start(f32[512]{0:T(512)} %param.5) | copy-start | bytes 6148
  46.2 65.8 %collective-permute-start = (bf16[2,512,1280]{2,1,0:T(8,128)(2,1)}, bf16[2,512,1280]{2,1,0:T(8,128)(2,1)}, u32[]{:S(2)}, u32[]{:S(2)}) collective-permute-start(bf16[2,512,1280]{2,1,0:T(8,128)(2,1)} %copy.25), channel_id=1, source_target_pairs={{0,4},{4,8},{8,12},{12,16},{16,20},{20,24},{24,28},{28,32},{32,36}... | collective-permute-start | bytes 7864328 | tf_op jit(solution)/shard_map/ppermute | solution.py:13
  112.0 63.7 %collective-permute-start.1 = (bf16[2,512,1280]{2,1,0:T(8,128)(2,1)}, bf16[2,512,1280]{2,1,0:T(8,128)(2,1)}, u32[]{:S(2)}, u32[]{:S(2)}) collective-permute-start(bf16[2,512,1280]{2,1,0:T(8,128)(2,1)} %collective-permute-done), channel_id=1, source_target_pairs={{0,4},{4,8},{8,12},{12,16},{16,20},{20,24},{24,28},{28,32},{32,36}... | collective-permute-start | bytes 7864328 | tf_op jit(solution)/shard_map/ppermute | solution.py:13
  112.0 2.2 copy-start.1
  199.9 4.6 copy-start.6
  199.9 4.6 copy-start.4
  199.9 5.9 copy-start.2
  200.0 4.6 copy-start.7
  208.1 393.1 %all-reduce.5.cloned.1.call-start = ((), (), s32[]{:S(2)}) async-start(), calls=%async_computation.2 | async-start | bytes 2097152 | tf_op jit(solution)/shard_map/psum | solution.py:52
  208.4 7.0 %copy-start.5 = (bf16[2,2,512,512]{3,2,0,1:T(8,128)(2,1)S(1)}, bf16[2,2,512,512]{3,2,0,1:T(8,128)(2,1)}, u32[]{:S(2)}) copy-start(bf16[2,2,512,512]{3,2,0,1:T(8,128)(2,1)} %copy-done.4) | copy-start | bytes 6291460
  215.3 28.0 %copy-start.3 = (bf16[2,2,512,512]{3,2,0,1:T(8,128)(2,1)S(1)}, bf16[2,2,512,512]{3,2,0,1:T(8,128)(2,1)}, u32[]{:S(2)}) copy-start(bf16[2,2,512,512]{3,2,0,1:T(8,128)(2,1)} %copy-done.2) | copy-start | bytes 6291460
Sparse Core Ops, SparseCore 0:
  208.3 35.0 all-reduce.2
  245.8 355.3 all-reduce.4
